TPU v7x, 32 devices: a whole 2x2x4 slice. The times are simulated.
32 devices in a mesh: layer: 8 (over y, x, core), lat: 4 (over z).
Axes of the slice: x: 2, y: 2, z: 4, core: 2. Of those that a mesh axis runs over, the one named last changes fastest.
Arguments:
- activations: bfloat16 [1536, 4096], P('layer', 'lat'), may hold values from -6 to 6
- w_enc: bfloat16 [1536, 8192], P('layer', 'lat'), may hold values from -0.15625 to 0.15625
- w_dec: bfloat16 [1536, 8192], P('layer', 'lat'), may hold values from -0.25 to 0.25
- b_enc: bfloat16 [8192], P('lat'), may hold values from -3 to 3
- b_dec: float32 [1536], P('layer'), may hold values from -3 to 3
- tile_ids: int32 [4, 4], replicated, may hold values from -1 to 63, as said below
Outputs:
- d_w_enc: bfloat16 [1536, 8192], P('layer', 'lat')
- d_w_dec: bfloat16 [1536, 8192], P('layer', 'lat')
- d_b_enc: float32 [8192], P('lat')
Inputs may be any that keep to these rules, and one draw needn't show every extreme that they name: `tile_ids`: row b lists the tiles of block b: live ids first, then -1. Live ids of a row are distinct, and no two of them share an owner id // 16. Each row has at least half of 4 (rounded up) live slots; some row has 4. One owner is named in every row.
All inputs are finite; a program needn't handle non-finite values.
Results may differ from a plain program's by a relative error of at most 0.02.
The roundings to bfloat16 on the way count: a program that leaves them out, or rounds other values in their place, can miss the bound.
Values may be sent and summed in bfloat16 or wider, within the bound.
No kernel may reach another device: no remote copies, remote signals or barrier semaphores. Data moves between devices by JAX's collectives and lax.ppermute only.
A program may use at most 64 MiB of HBM per device.

v0:
```python
import math
import jax
import jax.numpy as jnp
from jax import lax
from jax.sharding import PartitionSpec as P

TILE = 128


def rounded(value):
    return lax.optimization_barrier(value.astype(jnp.bfloat16)).astype(jnp.float32)


def local(activations, w_enc, w_dec, b_enc, b_dec, tile_ids):
    feature_count, row_count = activations.shape
    latent_count = w_enc.shape[1]
    owner_count = lax.axis_size("lat")
    tile_count = latent_count // TILE
    position = lax.axis_index("lat")
    owner_ids = jnp.where(tile_ids >= 0, tile_ids // tile_count, -1)
    matched = owner_ids == position
    local_tile = jnp.sum(jnp.where(matched, tile_ids % tile_count, 0), axis=1)
    wanted = jnp.any(matched, axis=1)
    chosen = (local_tile[:, None] == jnp.arange(tile_count)[None, :]) & wanted[:, None]
    chosen_half = chosen.astype(jnp.bfloat16)
    enc_table = w_enc.reshape(feature_count, tile_count, TILE)
    dec_table = w_dec.reshape(feature_count, tile_count, TILE)
    bias_table = b_enc.reshape(tile_count, TILE)
    enc_send = jnp.einsum(
        "rt,ftc->rfc", chosen_half, enc_table, preferred_element_type=jnp.float32
    ).astype(jnp.bfloat16)
    dec_send = jnp.einsum(
        "rt,ftc->rfc", chosen_half, dec_table, preferred_element_type=jnp.float32
    ).astype(jnp.bfloat16)
    bias_send = jnp.dot(chosen_half, bias_table, preferred_element_type=jnp.float32).astype(
        jnp.bfloat16
    )
    enc_recv, dec_recv, bias_recv = (
        lax.all_to_all(enc_send, "lat", split_axis=0, concat_axis=0, tiled=True),
        lax.all_to_all(dec_send, "lat", split_axis=0, concat_axis=0, tiled=True),
        lax.all_to_all(bias_send, "lat", split_axis=0, concat_axis=0, tiled=True),
    )
    my_list = lax.dynamic_index_in_dim(tile_ids, position, 0, keepdims=False)
    live_slot = my_list >= 0
    source = jnp.where(live_slot, my_list // tile_count, 0)
    live_half = live_slot.astype(jnp.bfloat16)
    live_float = live_slot.astype(jnp.float32)
    enc_cols = jnp.take(enc_recv, source, axis=0) * live_half[:, None, None]
    bias_cols = jnp.take(bias_recv, source, axis=0).astype(jnp.float32)
    partial_value = rounded(
        jnp.einsum("fr,kfc->rkc", activations, enc_cols, preferred_element_type=jnp.float32)
    )
    preact = lax.psum(partial_value, "layer") + bias_cols[None]
    latent_codes = (jax.nn.relu(preact) * live_float[None, :, None]).astype(jnp.bfloat16)
    dec_cols = jnp.take(dec_recv, source, axis=0) * live_half[:, None, None]
    rebuilt = (
        jnp.einsum("rkc,kfc->fr", latent_codes, dec_cols, preferred_element_type=jnp.float32)
        + b_dec[:, None]
    )
    residual = rebuilt - activations.astype(jnp.float32)
    grad_err = (residual / math.sqrt(row_count)).astype(jnp.bfloat16)
    dec_grad = jnp.einsum(
        "fr,rkc->kfc", grad_err, latent_codes, preferred_element_type=jnp.float32
    ).astype(jnp.bfloat16)
    back_part = rounded(
        jnp.einsum("fr,kfc->rkc", grad_err, dec_cols, preferred_element_type=jnp.float32)
    )
    grad_total = lax.psum(back_part, "layer")
    code_grad = (grad_total * (latent_codes > 0)).astype(jnp.bfloat16)
    enc_grad = jnp.einsum(
        "fr,rkc->kfc", activations, code_grad, preferred_element_type=jnp.float32
    ).astype(jnp.bfloat16)
    bias_grad = jnp.sum(code_grad, axis=0, dtype=jnp.float32).astype(jnp.bfloat16)
    placement = ((source[:, None] == jnp.arange(owner_count)[None, :]) & live_slot[:, None]).astype(
        jnp.bfloat16
    )
    enc_return = jnp.einsum(
        "ko,kfc->ofc", placement, enc_grad, preferred_element_type=jnp.float32
    ).astype(jnp.bfloat16)
    dec_return = jnp.einsum(
        "ko,kfc->ofc", placement, dec_grad, preferred_element_type=jnp.float32
    ).astype(jnp.bfloat16)
    bias_return = jnp.einsum(
        "ko,kc->oc", placement, bias_grad, preferred_element_type=jnp.float32
    ).astype(jnp.bfloat16)
    enc_got, dec_got, bias_got = (
        lax.all_to_all(enc_return, "lat", split_axis=0, concat_axis=0, tiled=True),
        lax.all_to_all(dec_return, "lat", split_axis=0, concat_axis=0, tiled=True),
        lax.all_to_all(bias_return, "lat", split_axis=0, concat_axis=0, tiled=True),
    )
    d_w_enc = (
        jnp.einsum("rt,rfc->ftc", chosen_half, enc_got, preferred_element_type=jnp.float32)
        .reshape(feature_count, latent_count)
        .astype(jnp.bfloat16)
    )
    d_w_dec = (
        jnp.einsum("rt,rfc->ftc", chosen_half, dec_got, preferred_element_type=jnp.float32)
        .reshape(feature_count, latent_count)
        .astype(jnp.bfloat16)
    )
    d_b_enc = jnp.einsum(
        "rt,rc->tc", chosen_half, bias_got, preferred_element_type=jnp.float32
    ).reshape(latent_count)
    return (d_w_enc, d_w_dec, d_b_enc)


def solution(mesh):
    return jax.shard_map(
        local,
        mesh=mesh,
        in_specs=(
            P("layer", "lat"),
            P("layer", "lat"),
            P("layer", "lat"),
            P("lat"),
            P("layer"),
            P(),
        ),
        out_specs=(P("layer", "lat"), P("layer", "lat"), P("lat")),
        check_vma=False,
    )
```

profile of v0, /device:TPU:0, one launch (start us, length us, event | category | flops | bytes accessed | tf_op | source)
XLA Modules:
  0.0 188.2 jit_solution(17841347270297134224)
XLA Ops:
  7.2 0.9 fusion.44
  8.1 0.8 fusion.23
  9.1 0.6 copy.46
  9.7 6.3 %all-to-all-start.1 = ((bf16[4,1,128]{2,1,0:T(2,128)(2,1)}), bf16[4,1,128]{2,1,0:T(2,128)(2,1)S(1)}, u32[]{:S(2)}, u32[]{:S(2)}) async-start(bf16[4,1,128]{2,1,0:T(2,128)(2,1)} %copy.46), calls=%async_computation.1 | async-start | bytes 4096 | tf_op jit(solution)/shard_map/all_to_all | solution.py:41
  16.0 0.7 fusion.42
  16.7 0.7 compare_and_fusion
  17.5 1.3 copy.65
  19.5 0.7 fusion.35
  20.2 0.7 copy.45
  20.9 0.7 copy.47
  21.6 5.1 %all-to-all-start = ((bf16[4,192,128]{2,1,0:T(8,128)(2,1)}), bf16[4,192,128]{2,1,0:T(8,128)(2,1)S(1)}, u32[]{:S(2)}, u32[]{:S(2)}) async-start(bf16[4,192,128]{2,1,0:T(8,128)(2,1)} %copy.45), calls=%async_computation | async-start | bytes 393216 | tf_op jit(solution)/shard_map/all_to_all | solution.py:39
  27.3 6.6 %all-to-all-done = bf16[4,192,128]{2,1,0:T(8,128)(2,1)S(1)} async-done(((bf16[4,192,128]{2,1,0:T(8,128)(2,1)}), bf16[4,192,128]{2,1,0:T(8,128)(2,1)S(1)}, u32[]{:S(2)}, u32[]{:S(2)}) %all-to-all-start) | async-done | bytes 196640 | tf_op jit(solution)/shard_map/all_to_all | solution.py:39
  34.0 3.4 %all-to-all-start.2 = ((bf16[4,192,128]{2,1,0:T(8,128)(2,1)}), bf16[4,192,128]{2,1,0:T(8,128)(2,1)S(1)}, u32[]{:S(2)}, u32[]{:S(2)}) async-start(bf16[4,192,128]{2,1,0:T(8,128)(2,1)} %copy.47), calls=%async_computation.2 | async-start | bytes 393216 | tf_op jit(solution)/shard_map/all_to_all | solution.py:40
  37.4 0.6 gather_fusion.1
  38.6 56.5 %all-reduce.4 = f32[1024,4,128]{0,2,1:T(8,128)S(1)} all-reduce(bf16[1024,4,128]{0,2,1:T(8,128)(2,1)S(1)} %fusion), channel_id=1, replica_groups=mesh['layer'=8,'lat'=4] {'layer'}, use_global_device_ids=true, to_apply=%region_2.4 | all-reduce | flops 524288 | bytes 3145728 | tf_op jit(solution)/shard_map/psum | solution.py:53
  95.4 1.2 gather_fusion.2
  96.7 1.6 fusion.5
  98.3 1.6 convolution_convert_fusion
  100.4 1.0 convolution_convert_fusion.8
  101.4 0.7 copy.56
  102.1 5.0 %all-to-all-start.4 = ((bf16[4,192,128]{2,1,0:T(8,128)(2,1)}), bf16[4,192,128]{2,1,0:T(8,128)(2,1)S(1)}, u32[]{:S(2)}, u32[]{:S(2)}) async-start(bf16[4,192,128]{2,1,0:T(8,128)(2,1)} %copy.56), calls=%async_computation.4 | async-start | bytes 393216 | tf_op jit(solution)/shard_map/all_to_all | solution.py:88
  107.1 49.9 %all-reduce.3.cloned.1.call-done = bf16[1024,4,128]{0,2,1:T(8,128)(2,1)} async-done(((bf16[1024,4,128]{0,2,1:T(8,128)(2,1)}), bf16[1024,4,128]{0,2,1:T(8,128)(2,1)}) %all-reduce.3.cloned.1.call-update) | async-done | bytes 1048592 | tf_op jit(solution)/shard_map/psum | solution.py:68
  157.0 2.0 %fusion.41 = bf16[4,128]{1,0:T(4,128)(2,1)S(1)} fusion(bf16[1024,4,128]{0,2,1:T(8,128)(2,1)} %all-reduce.3.cloned.1.call-done, f32[4]{0:T(128)S(1)} %copy-done.9, f32[1024,4,128]{0,2,1:T(8,128)S(1)} %all-reduce.4, f32[4,128]{1,0:T(4,128)S(1)} %select_convert_fusion.1), kind=kLoop, calls=%fused_computation.90 | loop fusion | flops 4718080 | bytes 3148816 | tf_op jit(solution)/shard_map/reduce_sum | solution.py:73
  159.1 0.6 copy.58
  160.2 4.5 %all-to-all-start.5 = ((bf16[4,1,128]{2,1,0:T(2,128)(2,1)}), bf16[4,1,128]{2,1,0:T(2,128)(2,1)S(1)}, u32[]{:S(2)}, u32[]{:S(2)}) async-start(bf16[4,1,128]{2,1,0:T(2,128)(2,1)} %copy.58), calls=%async_computation.5 | async-start | bytes 4096 | tf_op jit(solution)/shard_map/all_to_all | solution.py:89
  165.0 0.7 copy.52
  165.7 4.5 %all-to-all-done.5 = bf16[4,1,128]{2,1,0:T(2,128)(2,1)S(1)} async-done(((bf16[4,1,128]{2,1,0:T(2,128)(2,1)}), bf16[4,1,128]{2,1,0:T(2,128)(2,1)S(1)}, u32[]{:S(2)}, u32[]{:S(2)}) %all-to-all-start.5) | async-done | bytes 1056 | tf_op jit(solution)/shard_map/all_to_all | solution.py:89
  170.2 3.4 %all-to-all-start.3 = ((bf16[4,192,128]{2,1,0:T(8,128)(2,1)}), bf16[4,192,128]{2,1,0:T(8,128)(2,1)S(1)}, u32[]{:S(2)}, u32[]{:S(2)}) async-start(bf16[4,192,128]{2,1,0:T(8,128)(2,1)} %copy.52), calls=%async_computation.3 | async-start | bytes 393216 | tf_op jit(solution)/shard_map/all_to_all | solution.py:87
  174.0 1.1 copy.84
  175.1 0.8 convolution_bitcast_fusion.1
  175.9 3.9 %all-to-all-done.3 = bf16[4,192,128]{2,1,0:T(8,128)(2,1)S(1)} async-done(((bf16[4,192,128]{2,1,0:T(8,128)(2,1)}), bf16[4,192,128]{2,1,0:T(8,128)(2,1)S(1)}, u32[]{:S(2)}, u32[]{:S(2)}) %all-to-all-start.3) | async-done | bytes 196640 | tf_op jit(solution)/shard_map/all_to_all | solution.py:87
  180.2 1.1 copy.85
  (52 shorter events, 4.7 us)
Async XLA Ops:
  7.2 1.8 copy-start
  7.2 11.8 %copy-start.2 = (bf16[192,2048]{1,0:T(8,128)(2,1)S(1)}, bf16[192,2048]{1,0:T(8,128)(2,1)}, u32[]{:S(2)}) copy-start(bf16[192,2048]{1,0:T(8,128)(2,1)} %param.10) | copy-start | bytes 2359300
  9.7 11.9 %all-to-all-start.1 = ((bf16[4,1,128]{2,1,0:T(2,128)(2,1)}), bf16[4,1,128]{2,1,0:T(2,128)(2,1)S(1)}, u32[]{:S(2)}, u32[]{:S(2)}) async-start(bf16[4,1,128]{2,1,0:T(2,128)(2,1)} %copy.46), calls=%async_computation.1 | async-start | bytes 4096 | tf_op jit(solution)/shard_map/all_to_all | solution.py:41
  16.7 2.8 %copy-start.10 = (pred[4]{0:T(512)(128)(4,1)}, pred[4]{0:T(512)(128)(4,1)S(1)}, u32[]{:S(2)}) copy-start(pred[4]{0:T(512)(128)(4,1)S(1)} %get-tuple-element.5) | copy-start | bytes 16
  16.7 78.4 %copy-start.8 = (f32[4]{0:T(128)}, f32[4]{0:T(128)S(1)}, u32[]{:S(2)}) copy-start(f32[4]{0:T(128)S(1)} %get-tuple-element.4) | copy-start | bytes 52
  17.4 1.8 copy-start.12
  17.4 78.0 %copy-start.6 = (bf16[4]{0:T(256)(128)(2,1)}, bf16[4]{0:T(256)(128)(2,1)S(1)}, u32[]{:S(2)}) copy-start(bf16[4]{0:T(256)(128)(2,1)S(1)} %get-tuple-element.10) | copy-start | bytes 28
  19.0 19.0 %copy-start.4 = (bf16[192,1024]{1,0:T(8,128)(2,1)S(1)}, bf16[192,1024]{1,0:T(8,128)(2,1)}, u32[]{:S(2)}) copy-start(bf16[192,1024]{1,0:T(8,128)(2,1)} %param.8) | copy-start | bytes 1179652
  21.6 12.4 %all-to-all-start = ((bf16[4,192,128]{2,1,0:T(8,128)(2,1)}), bf16[4,192,128]{2,1,0:T(8,128)(2,1)S(1)}, u32[]{:S(2)}, u32[]{:S(2)}) async-start(bf16[4,192,128]{2,1,0:T(8,128)(2,1)} %copy.45), calls=%async_computation | async-start | bytes 393216 | tf_op jit(solution)/shard_map/all_to_all | solution.py:39
  34.0 61.4 %all-to-all-start.2 = ((bf16[4,192,128]{2,1,0:T(8,128)(2,1)}), bf16[4,192,128]{2,1,0:T(8,128)(2,1)S(1)}, u32[]{:S(2)}, u32[]{:S(2)}) async-start(bf16[4,192,128]{2,1,0:T(8,128)(2,1)} %copy.47), calls=%async_computation.2 | async-start | bytes 393216 | tf_op jit(solution)/shard_map/all_to_all | solution.py:40
  37.3 119.6 %all-reduce.3.cloned.1.call-start = ((), (), s32[]{:S(2)}) async-start(), calls=%async_computation.6 | async-start | bytes 2097152 | tf_op jit(solution)/shard_map/psum | solution.py:68
  96.7 1.6 copy-start.3
  96.7 1.6 copy-start.7
  99.9 57.1 %copy-start.9 = (f32[4]{0:T(128)S(1)}, f32[4]{0:T(128)}, u32[]{:S(2)}) copy-start(f32[4]{0:T(128)} %copy-done.8) | copy-start | bytes 52
  100.4 58.5 %copy-start.11 = (pred[4]{0:T(512)(128)(4,1)S(1)}, pred[4]{0:T(512)(128)(4,1)}, u32[]{:S(2)}) copy-start(pred[4]{0:T(512)(128)(4,1)} %copy-done.10) | copy-start | bytes 16
  100.4 58.5 %copy-start.13 = (s32[4]{0:T(128)S(1)}, s32[4]{0:T(128)}, u32[]{:S(2)}) copy-start(s32[4]{0:T(128)} %copy-done.12) | copy-start | bytes 52
  102.1 58.1 %all-to-all-start.4 = ((bf16[4,192,128]{2,1,0:T(8,128)(2,1)}), bf16[4,192,128]{2,1,0:T(8,128)(2,1)S(1)}, u32[]{:S(2)}, u32[]{:S(2)}) async-start(bf16[4,192,128]{2,1,0:T(8,128)(2,1)} %copy.56), calls=%async_computation.4 | async-start | bytes 393216 | tf_op jit(solution)/shard_map/all_to_all | solution.py:88
  156.9 2.7 %copy-start.1 = (bf16[1024,4,128]{0,2,1:T(8,128)(2,1)S(1)}, bf16[1024,4,128]{0,2,1:T(8,128)(2,1)}, u32[]{:S(2)}) copy-start(bf16[1024,4,128]{0,2,1:T(8,128)(2,1)} %all-reduce.3.cloned.1.call-done) | copy-start | bytes 3145732
  156.9 2.7 %copy-start.5 = (bf16[192,1024]{1,0:T(8,128)(2,1)S(1)}, bf16[192,1024]{1,0:T(8,128)(2,1)}, u32[]{:S(2)}) copy-start(bf16[192,1024]{1,0:T(8,128)(2,1)} %param.8) | copy-start | bytes 1179652
  160.2 10.0 %all-to-all-start.5 = ((bf16[4,1,128]{2,1,0:T(2,128)(2,1)}), bf16[4,1,128]{2,1,0:T(2,128)(2,1)S(1)}, u32[]{:S(2)}, u32[]{:S(2)}) async-start(bf16[4,1,128]{2,1,0:T(2,128)(2,1)} %copy.58), calls=%async_computation.5 | async-start | bytes 4096 | tf_op jit(solution)/shard_map/all_to_all | solution.py:89
  170.2 9.6 %all-to-all-start.3 = ((bf16[4,192,128]{2,1,0:T(8,128)(2,1)}), bf16[4,192,128]{2,1,0:T(8,128)(2,1)S(1)}, u32[]{:S(2)}, u32[]{:S(2)}) async-start(bf16[4,192,128]{2,1,0:T(8,128)(2,1)} %copy.52), calls=%async_computation.3 | async-start | bytes 393216 | tf_op jit(solution)/shard_map/all_to_all | solution.py:87
Sparse Core Ops, SparseCore 0:
  100.0 56.8 all-reduce.2
where the time goes:
time: 189 us; the launch traced here: 188 us
  waiting for transfers between devices  65 us (34%)
  blocking collectives  56.5 us (30%)
  starting transfers between devices  27.7 us (15%)
  between operations  14.3 us (8%)
  local copies, waits for them, and re-layouts  10.1 us (5%)
  matrix products  8.36 us (4%)
  other arithmetic  6.22 us (3%)
    psum x1, blocking collectives, local(): preact = lax.psum(partial_value, 'layer') + bias_cols[None]  56.5 us
    psum x1, waiting for transfers between devices, local(): grad_total = lax.psum(back_part, 'layer')  49.9 us
    all_to_all x1, waiting for transfers between devices, local(): lax.all_to_all(enc_send, 'lat', split_axis=0, concat_axis=0, tiled=True)  6.63 us
    all_to_all x1, starting transfers between devices, local(): lax.all_to_all(bias_send, 'lat', split_axis=0, concat_axis=0, tiled=True)  6.35 us
    all_to_all x1, starting transfers between devices, local(): lax.all_to_all(enc_send, 'lat', split_axis=0, concat_axis=0, tiled=True)  5.09 us
    all_to_all x1, starting transfers between devices, local(): lax.all_to_all(dec_return, 'lat', split_axis=0, concat_axis=0, tiled=True)  4.97 us
    all_to_all x1, starting transfers between devices, local(): lax.all_to_all(bias_return, 'lat', split_axis=0, concat_axis=0, tiled=True)  4.55 us
    all_to_all x1, waiting for transfers between devices, local(): lax.all_to_all(bias_return, 'lat', split_axis=0, concat_axis=0, tiled=True)  4.53 us
  transfers between devices with their start and end apart: 7, of which 4 were waited for; matrix products, arithmetic and copies ran while one was open for 9% of the time, Pallas kernels for 0%

commit v1 on v0

--- a/solution.py
+++ b/solution.py
@@ -5,6 +5,7 @@
 from jax.sharding import PartitionSpec as P
 
 TILE = 128
+sector_draw = lambda inner_x: lax.all_gather(inner_x, axis_name="layer").sum(axis=0)
 
 
 def rounded(value):
@@ -50,7 +51,7 @@
     partial_value = rounded(
         jnp.einsum("fr,kfc->rkc", activations, enc_cols, preferred_element_type=jnp.float32)
     )
-    preact = lax.psum(partial_value, "layer") + bias_cols[None]
+    preact = sector_draw(partial_value) + bias_cols[None]
     latent_codes = (jax.nn.relu(preact) * live_float[None, :, None]).astype(jnp.bfloat16)
     dec_cols = jnp.take(dec_recv, source, axis=0) * live_half[:, None, None]
     rebuilt = (

time: 189 us -> 243 us (1.29)
  waiting for transfers between devices: 65 us -> 143 us
  blocking collectives: 56.5 us -> 0 us
  local copies, waits for them, and re-layouts: 10.1 us -> 34.3 us
  other arithmetic: 6.22 us -> 16.5 us
    all_gather x0 -> x1, waiting for transfers between devices: none -> 68.7 us  [lax.all_gather(inner_x, axis_name='layer').sum(axis=0)]
    psum x1 -> x0, blocking collectives: 56.5 us -> none  [local(): preact = lax.psum(partial_value, 'layer') + bias_cols[None]]
    unnamed x33 -> x38, local copies, waits for them, and re-layouts: 3.68 us -> 26.1 us
    reduce_sum x0 -> x1, other arithmetic: none -> 9.65 us  [lax.all_gather(inner_x, axis_name='layer').sum(axis=0)]
    all_to_all x1, waiting for transfers between devices: 0.01 us -> 5.5 us  [local(): lax.all_to_all(dec_send, 'lat', split_axis=0, concat_axis=0, tiled=True)]
    all_to_all x1, waiting for transfers between devices: 0.01 us -> 4.3 us  [local(): lax.all_to_all(bias_send, 'lat', split_axis=0, concat_axis=0, tiled=True)]
    all_to_all x1, starting transfers between devices: 6.35 us -> 3.22 us  [local(): lax.all_to_all(bias_send, 'lat', split_axis=0, concat_axis=0, tiled=True)]
  transfers between devices with their start and end apart: 7 -> 8, of which waited for: 4 -> 7; matrix products, arithmetic and copies ran while one was open for 9% -> 6% of each run, Pallas kernels for 0% -> 0%
where the time goes in v1:
time: 243 us; the launch traced here: 242 us
  waiting for transfers between devices  143 us (59%)
  local copies, waits for them, and re-layouts  34.3 us (14%)
  starting transfers between devices  25.5 us (10%)
  other arithmetic  16.5 us (7%)
  between operations  14.4 us (6%)
  matrix products  8.55 us (4%)
    all_gather x1, waiting for transfers between devices, lax.all_gather(inner_x, axis_name='layer').sum(axis=0)  68.7 us
    psum x1, waiting for transfers between devices, local(): grad_total = lax.psum(back_part, 'layer')  49.3 us
    unnamed x38, local copies, waits for them, and re-layouts  26.1 us
    reduce_sum x1, other arithmetic, lax.all_gather(inner_x, axis_name='layer').sum(axis=0)  9.65 us
    all_to_all x1, waiting for transfers between devices, local(): lax.all_to_all(enc_send, 'lat', split_axis=0, concat_axis=0, tiled=True)  6.44 us
    all_to_all x1, starting transfers between devices, local(): lax.all_to_all(enc_send, 'lat', split_axis=0, concat_axis=0, tiled=True)  6.35 us
    all_to_all x1, waiting for transfers between devices, local(): lax.all_to_all(dec_send, 'lat', split_axis=0, concat_axis=0, tiled=True)  5.5 us
  transfers between devices with their start and end apart: 8, of which 7 were waited for; matrix products, arithmetic and copies ran while one was open for 6% of the time, Pallas kernels for 0%

profile of v1, /device:TPU:0, one launch (start us, length us, event | category | flops | bytes accessed | tf_op | source)
XLA Modules:
  0.0 242.0 jit_solution(9959865610316527451)
XLA Ops:
  7.2 0.9 fusion.44
  8.1 0.8 fusion.23
  8.9 1.3 copy.48
  10.5 0.7 copy.35
  11.2 6.3 %all-to-all-start = ((bf16[4,192,128]{2,1,0:T(8,128)(2,1)}), bf16[4,192,128]{2,1,0:T(8,128)(2,1)S(1)}, u32[]{:S(2)}, u32[]{:S(2)}) async-start(bf16[4,192,128]{2,1,0:T(8,128)(2,1)} %copy.35), calls=%async_computation | async-start | bytes 393216 | tf_op jit(solution)/shard_map/all_to_all | solution.py:40
  18.6 6.4 %all-to-all-done = bf16[4,192,128]{2,1,0:T(8,128)(2,1)S(1)} async-done(((bf16[4,192,128]{2,1,0:T(8,128)(2,1)}), bf16[4,192,128]{2,1,0:T(8,128)(2,1)S(1)}, u32[]{:S(2)}, u32[]{:S(2)}) %all-to-all-start) | async-done | bytes 196640 | tf_op jit(solution)/shard_map/all_to_all | solution.py:40
  26.3 1.6 all_gather.12
  28.6 3.2 %all-to-all-start.1 = ((bf16[4,1,128]{2,1,0:T(2,128)(2,1)}), bf16[4,1,128]{2,1,0:T(2,128)(2,1)S(1)}, u32[]{:S(2)}, u32[]{:S(2)}) async-start(bf16[4,1,128]{2,1,0:T(2,128)(2,1)} %copy.36), calls=%async_computation.1 | async-start | bytes 4096 | tf_op jit(solution)/shard_map/all_to_all | solution.py:42
  33.0 4.3 %all-to-all-done.1 = bf16[4,1,128]{2,1,0:T(2,128)(2,1)S(1)} async-done(((bf16[4,1,128]{2,1,0:T(2,128)(2,1)}), bf16[4,1,128]{2,1,0:T(2,128)(2,1)S(1)}, u32[]{:S(2)}, u32[]{:S(2)}) %all-to-all-start.1) | async-done | bytes 1056 | tf_op jit(solution)/shard_map/all_to_all | solution.py:42
  37.3 3.4 %all-to-all-start.2 = ((bf16[4,192,128]{2,1,0:T(8,128)(2,1)}), bf16[4,192,128]{2,1,0:T(8,128)(2,1)S(1)}, u32[]{:S(2)}, u32[]{:S(2)}) async-start(bf16[4,192,128]{2,1,0:T(8,128)(2,1)} %copy.38), calls=%async_computation.2 | async-start | bytes 393216 | tf_op jit(solution)/shard_map/all_to_all | solution.py:41
  41.4 5.5 %all-to-all-done.2 = bf16[4,192,128]{2,1,0:T(8,128)(2,1)S(1)} async-done(((bf16[4,192,128]{2,1,0:T(8,128)(2,1)}), bf16[4,192,128]{2,1,0:T(8,128)(2,1)S(1)}, u32[]{:S(2)}, u32[]{:S(2)}) %all-to-all-start.2) | async-done | bytes 196640 | tf_op jit(solution)/shard_map/all_to_all | solution.py:41
  46.9 1.2 gather_fusion.2
  48.1 68.7 %all-gather.3.cloned.1.call-done = f32[8192,4,128]{0,2,1:T(8,128)} async-done(((f32[1024,4,128]{0,2,1:T(8,128)}), f32[8192,4,128]{0,2,1:T(8,128)}) %all-gather.3.cloned.1.call-update) | async-done | bytes 16777232 | tf_op jit(solution)/shard_map/all_gather | solution.py:8
  116.8 21.2 %copy.49 = f32[64,8,8,1024]{3,2,1,0:T(8,128)} copy(f32[64,8,8,1024]{3,1,2,0:T(8,128)} %bitcast.109) | data formatting | bytes 33554432
  138.0 9.7 %reduce_sum.31 = f32[1024,4,128]{0,2,1:T(8,128)} reduce(f32[8,1024,4,128]{1,0,3,2:T(8,128)} %bitcast.108, f32[]{:T(128)} %constant.81.clone.1), dimensions={0}, to_apply=%region_2.4 | reduce | flops 3670016 | bytes 18874372 | tf_op jit(solution)/shard_map/reduce_sum | solution.py:8
  147.6 1.9 copy.37
  149.6 1.0 multiply_convert_fusion
  151.1 0.7 copy-done.5
  151.9 1.5 convolution_convert_fusion
  153.4 1.4 fusion.7
  154.8 0.9 convolution_convert_fusion.8
  156.4 4.6 %all-to-all-start.4 = ((bf16[4,192,128]{2,1,0:T(8,128)(2,1)}), bf16[4,192,128]{2,1,0:T(8,128)(2,1)S(1)}, u32[]{:S(2)}, u32[]{:S(2)}) async-start(bf16[4,192,128]{2,1,0:T(8,128)(2,1)} %copy.43), calls=%async_computation.4 | async-start | bytes 393216 | tf_op jit(solution)/shard_map/all_to_all | solution.py:89
  161.0 49.3 %all-reduce.2.cloned.1.call-done = bf16[1024,4,128]{2,0,1:T(8,128)(2,1)} async-done(((bf16[1024,4,128]{2,0,1:T(8,128)(2,1)}), bf16[1024,4,128]{2,0,1:T(8,128)(2,1)}) %all-reduce.2.cloned.1.call-update) | async-done | bytes 1048592 | tf_op jit(solution)/shard_map/psum | solution.py:69
  210.3 1.9 fusion.41
  212.2 0.8 fusion.9
  214.0 4.5 %all-to-all-start.5 = ((bf16[4,1,128]{2,1,0:T(2,128)(2,1)}), bf16[4,1,128]{2,1,0:T(2,128)(2,1)S(1)}, u32[]{:S(2)}, u32[]{:S(2)}) async-start(bf16[4,1,128]{2,1,0:T(2,128)(2,1)} %copy.45), calls=%async_computation.5 | async-start | bytes 4096 | tf_op jit(solution)/shard_map/all_to_all | solution.py:90
  219.5 4.5 %all-to-all-done.5 = bf16[4,1,128]{2,1,0:T(2,128)(2,1)S(1)} async-done(((bf16[4,1,128]{2,1,0:T(2,128)(2,1)}), bf16[4,1,128]{2,1,0:T(2,128)(2,1)S(1)}, u32[]{:S(2)}, u32[]{:S(2)}) %all-to-all-start.5) | async-done | bytes 1056 | tf_op jit(solution)/shard_map/all_to_all | solution.py:90
  224.0 3.4 %all-to-all-start.3 = ((bf16[4,192,128]{2,1,0:T(8,128)(2,1)}), bf16[4,192,128]{2,1,0:T(8,128)(2,1)S(1)}, u32[]{:S(2)}, u32[]{:S(2)}) async-start(bf16[4,192,128]{2,1,0:T(8,128)(2,1)} %copy.40), calls=%async_computation.3 | async-start | bytes 393216 | tf_op jit(solution)/shard_map/all_to_all | solution.py:88
  227.8 1.1 copy.69
  228.9 0.8 convolution_bitcast_fusion.1
  229.7 3.9 %all-to-all-done.3 = bf16[4,192,128]{2,1,0:T(8,128)(2,1)S(1)} async-done(((bf16[4,192,128]{2,1,0:T(8,128)(2,1)}), bf16[4,192,128]{2,1,0:T(8,128)(2,1)S(1)}, u32[]{:S(2)}, u32[]{:S(2)}) %all-to-all-start.3) | async-done | bytes 196640 | tf_op jit(solution)/shard_map/all_to_all | solution.py:88
  234.0 1.1 copy.70
  (62 shorter events, 9.2 us)
Async XLA Ops:
  7.2 20.7 %copy-start = (bf16[2048]{0:T(1024)(128)(2,1)S(1)}, bf16[2048]{0:T(1024)(128)(2,1)}, u32[]{:S(2)}) copy-start(bf16[2048]{0:T(1024)(128)(2,1)} %param.11) | copy-start | bytes 12292
  7.2 10.4 %copy-start.7 = (s32[4,4]{1,0:T(4,128)S(1)}, s32[4,4]{1,0:T(4,128)}, u32[]{:S(2)}) copy-start(s32[4,4]{1,0:T(4,128)} %param.13) | copy-start | bytes 196
  7.2 18.5 %copy-start.3 = (bf16[192,1024]{1,0:T(8,128)(2,1)S(1)}, bf16[192,1024]{1,0:T(8,128)(2,1)}, u32[]{:S(2)}) copy-start(bf16[192,1024]{1,0:T(8,128)(2,1)} %param.8) | copy-start | bytes 1179652
  11.2 13.9 %all-to-all-start = ((bf16[4,192,128]{2,1,0:T(8,128)(2,1)}), bf16[4,192,128]{2,1,0:T(8,128)(2,1)S(1)}, u32[]{:S(2)}, u32[]{:S(2)}) async-start(bf16[4,192,128]{2,1,0:T(8,128)(2,1)} %copy.35), calls=%async_computation | async-start | bytes 393216 | tf_op jit(solution)/shard_map/all_to_all | solution.py:40
  17.6 99.2 %all-gather.3.cloned.1.call-start = ((), (), s32[]{:S(2)}) async-start(), calls=%async_computation.7 | async-start | bytes 18874368 | tf_op jit(solution)/shard_map/all_gather | solution.py:8
  18.1 0.5 copy-start.11
  18.1 0.5 copy-start.13
  18.1 9.7 %copy-start.9 = (bf16[4]{0:T(256)(128)(2,1)}, bf16[4]{0:T(256)(128)(2,1)S(1)}, u32[]{:S(2)}) copy-start(bf16[4]{0:T(256)(128)(2,1)S(1)} %get-tuple-element.10) | copy-start | bytes 28
  26.2 5.6 %copy-start.2 = (bf16[192,2048]{1,0:T(8,128)(2,1)S(1)}, bf16[192,2048]{1,0:T(8,128)(2,1)}, u32[]{:S(2)}) copy-start(bf16[192,2048]{1,0:T(8,128)(2,1)} %param.10) | copy-start | bytes 2359300
  28.6 8.7 %all-to-all-start.1 = ((bf16[4,1,128]{2,1,0:T(2,128)(2,1)}), bf16[4,1,128]{2,1,0:T(2,128)(2,1)S(1)}, u32[]{:S(2)}, u32[]{:S(2)}) async-start(bf16[4,1,128]{2,1,0:T(2,128)(2,1)} %copy.36), calls=%async_computation.1 | async-start | bytes 4096 | tf_op jit(solution)/shard_map/all_to_all | solution.py:42
  37.3 9.6 %all-to-all-start.2 = ((bf16[4,192,128]{2,1,0:T(8,128)(2,1)}), bf16[4,192,128]{2,1,0:T(8,128)(2,1)S(1)}, u32[]{:S(2)}, u32[]{:S(2)}) async-start(bf16[4,192,128]{2,1,0:T(8,128)(2,1)} %copy.38), calls=%async_computation.2 | async-start | bytes 393216 | tf_op jit(solution)/shard_map/all_to_all | solution.py:41
  40.6 169.6 %all-reduce.2.cloned.1.call-start = ((), (), s32[]{:S(2)}) async-start(), calls=%async_computation.6 | async-start | bytes 2097152 | tf_op jit(solution)/shard_map/psum | solution.py:69
  149.5 1.0 copy-start.6
  149.5 1.0 copy-start.10
  149.5 1.0 copy-start.15
  151.1 0.7 copy-start.5
  153.4 56.9 %copy-start.8 = (f32[4]{0:T(128)S(1)}, f32[4]{0:T(128)}, u32[]{:S(2)}) copy-start(f32[4]{0:T(128)} %get-tuple-element.4) | copy-start | bytes 52
  156.4 57.6 %all-to-all-start.4 = ((bf16[4,192,128]{2,1,0:T(8,128)(2,1)}), bf16[4,192,128]{2,1,0:T(8,128)(2,1)S(1)}, u32[]{:S(2)}, u32[]{:S(2)}) async-start(bf16[4,192,128]{2,1,0:T(8,128)(2,1)} %copy.43), calls=%async_computation.4 | async-start | bytes 393216 | tf_op jit(solution)/shard_map/all_to_all | solution.py:89
  210.3 3.3 %copy-start.1 = (bf16[1024,4,128]{2,0,1:T(8,128)(2,1)S(1)}, bf16[1024,4,128]{2,0,1:T(8,128)(2,1)}, u32[]{:S(2)}) copy-start(bf16[1024,4,128]{2,0,1:T(8,128)(2,1)} %all-reduce.2.cloned.1.call-done) | copy-start | bytes 3145732
  210.3 3.3 %copy-start.4 = (bf16[192,1024]{1,0:T(8,128)(2,1)S(1)}, bf16[192,1024]{1,0:T(8,128)(2,1)}, u32[]{:S(2)}) copy-start(bf16[192,1024]{1,0:T(8,128)(2,1)} %param.8) | copy-start | bytes 1179652
  212.2 6.4 %copy-start.12 = (pred[4]{0:T(512)(128)(4,1)S(1)}, pred[4]{0:T(512)(128)(4,1)}, u32[]{:S(2)}) copy-start(pred[4]{0:T(512)(128)(4,1)} %copy-done.11) | copy-start | bytes 16
  212.2 6.4 %copy-start.14 = (s32[4]{0:T(128)S(1)}, s32[4]{0:T(128)}, u32[]{:S(2)}) copy-start(s32[4]{0:T(128)} %copy-done.13) | copy-start | bytes 52
  214.0 10.0 %all-to-all-start.5 = ((bf16[4,1,128]{2,1,0:T(2,128)(2,1)}), bf16[4,1,128]{2,1,0:T(2,128)(2,1)S(1)}, u32[]{:S(2)}, u32[]{:S(2)}) async-start(bf16[4,1,128]{2,1,0:T(2,128)(2,1)} %copy.45), calls=%async_computation.5 | async-start | bytes 4096 | tf_op jit(solution)/shard_map/all_to_all | solution.py:90
  224.0 9.6 %all-to-all-start.3 = ((bf16[4,192,128]{2,1,0:T(8,128)(2,1)}), bf16[4,192,128]{2,1,0:T(8,128)(2,1)S(1)}, u32[]{:S(2)}, u32[]{:S(2)}) async-start(bf16[4,192,128]{2,1,0:T(8,128)(2,1)} %copy.40), calls=%async_computation.3 | async-start | bytes 393216 | tf_op jit(solution)/shard_map/all_to_all | solution.py:88
Sparse Core Ops, SparseCore 0:
  28.0 88.7 all-gather.2
  153.5 56.7 all-reduce.1
